TPU v7x, 256 devices: a whole 4x4x8 slice. The times are simulated.
256 devices in a mesh: samples: 16 (over x, z_hi), genes: 8 (over z_lo, y), tissues: 2 (over core).
Axes of the slice: x: 4, y: 4, z: 8 (z_hi: 4, z_lo: 2; z = z_hi * 2 + z_lo), core: 2. Of those that a mesh axis runs over, the one named last changes fastest.
Arguments:
- dosage: bfloat16 [256, 8192, 128], P('genes', 'samples')
- traits: bfloat16 [8192, 256], P('samples'), may hold values from -6 to 6
- weights: bfloat16 [512, 48, 512], P('genes', 'tissues'), may hold values from -0.25 to 0.25
- block_mask: int32 [512, 48, 4], P('genes', 'tissues'), may hold values 0 or 1
- window_start: int32 [512], replicated, may hold values from 0 to 252, as said below
- precision_matrix: float32 [48, 48], replicated, as said below
Outputs:
- combined: float32 [512, 256], P('genes', 'samples')
- heterogeneity: float32 [512, 256], P('genes', 'samples')
Inputs may be any that keep to these rules, and one draw needn't show every extreme that they name: Gene g's cis window is the 4 consecutive blocks from window_start[g], all held by one device along genes (blocks b * 32 to (b + 1) * 32 - 1 on index b). Of the genes of one device along genes, at most 16 have their windows on one holder, and exactly 16 on some holder. `precision_matrix`: Symmetric, each diagonal entry larger than the sum of magnitudes off the diagonal in its row.
All inputs are finite; a program needn't handle non-finite values. No bound on the sum of `block_mask` on one device may be relied on, other than what follows from the above.
Results may differ from a plain program's by a relative error of at most 0.0029.
Values may be sent and summed in bfloat16 or wider, within the bound.
A program may use at most 192 MiB of HBM per device.

v0:
```python
import jax
import jax.numpy as jnp
from jax import lax
from jax.sharding import PartitionSpec as P

TISSUES = 48


def on_device(dosage, traits, weights, block_mask, window_start, precision_matrix):
    owner_count = lax.axis_size("genes")
    my_index = lax.axis_index("genes")
    block_count = dosage.shape[0]
    block_len = dosage.shape[2]
    gene_rows = weights.shape[0]
    tissue_cols = weights.shape[1]
    window_len = block_mask.shape[2]
    capacity = 2 * gene_rows // owner_count
    slot_count = owner_count * capacity
    genes_all = window_start.shape[0]
    sample_count = lax.axis_size("samples")
    trait_cols = traits.shape[1] // sample_count
    holder_all = window_start // block_count
    onehot = (holder_all[:, None] == jnp.arange(owner_count, dtype=jnp.int32)[None, :]).astype(
        jnp.int32
    )
    grouped = onehot.reshape(genes_all // gene_rows, gene_rows, owner_count)
    before = jnp.cumsum(grouped, axis=1) - grouped
    rank_all = jnp.sum(before * grouped, axis=2).reshape(genes_all)
    owner_all = jnp.arange(genes_all, dtype=jnp.int32) // gene_rows
    slot_all = holder_all * capacity + rank_all
    slot_mine = lax.dynamic_slice_in_dim(slot_all, my_index * gene_rows, gene_rows, 0)
    shaped = weights.reshape(gene_rows, tissue_cols, window_len, block_len)
    masked = (shaped * block_mask[..., None].astype(jnp.bfloat16)).reshape(
        gene_rows, tissue_cols, window_len * block_len
    )
    placer = (slot_mine[None, :] == jnp.arange(slot_count, dtype=jnp.int32)[:, None]).astype(
        jnp.bfloat16
    )
    outgoing = jnp.einsum("cj,jtx->ctx", placer, masked, preferred_element_type=jnp.float32).astype(
        jnp.bfloat16
    )
    target_all = owner_all * capacity + rank_all
    live_all = holder_all == my_index
    matches = (target_all[None, :] == jnp.arange(slot_count, dtype=jnp.int32)[:, None]) & live_all[
        None, :
    ]
    local_start = window_start - my_index * block_count
    slot_offset = jnp.sum(jnp.where(matches, local_start[None, :], 0), axis=1)
    arrived = lax.all_to_all(outgoing, "genes", split_axis=0, concat_axis=0, tiled=True)
    total = jnp.zeros((arrived.shape[0], arrived.shape[1], dosage.shape[1]), jnp.float32)
    for offset in range(window_len):
        blocks = jnp.take(dosage, slot_offset + offset, axis=0)
        piece = arrived[:, :, offset * block_len : (offset + 1) * block_len]
        total = total + jnp.einsum(
            "csv,ctv->cts", blocks, piece, preferred_element_type=jnp.float32
        )
    predicted = total.astype(jnp.bfloat16)
    replied = lax.all_to_all(predicted, "genes", split_axis=0, concat_axis=0, tiled=True)
    mine = jnp.take(replied, slot_mine, axis=0)
    flat = mine.reshape(gene_rows * tissue_cols, mine.shape[2])
    products = jnp.dot(flat, traits, preferred_element_type=jnp.float32).reshape(
        gene_rows, tissue_cols, traits.shape[1]
    )
    mine_wide = mine.astype(jnp.float32)
    squares = jnp.sum(mine_wide * mine_wide, axis=2)
    products, squares = lax.psum((products, squares), "samples")
    products = lax.dynamic_slice_in_dim(
        products, lax.axis_index("samples") * trait_cols, trait_cols, 2
    )
    scores = products / jnp.sqrt(squares[..., None] + 1.0)
    gathered = lax.all_gather(scores, "tissues", axis=1, tiled=True)
    row_sums = jnp.sum(precision_matrix, axis=1)
    grand_total = jnp.sum(row_sums)
    weighted = jnp.einsum(
        "tu,guk->gtk", precision_matrix, gathered, precision=lax.Precision.HIGHEST
    )
    linear = jnp.einsum("t,gtk->gk", row_sums, gathered, precision=lax.Precision.HIGHEST)
    quadratic = jnp.sum(gathered * weighted, axis=1)
    combined = linear / jnp.sqrt(grand_total)
    heterogeneity = (quadratic - linear * linear / grand_total) / TISSUES
    return (combined, heterogeneity)


def solution(mesh):
    in_specs = (
        P("genes", "samples", None),
        P("samples", None),
        P("genes", "tissues", None),
        P("genes", "tissues", None),
        P(),
        P(),
    )
    out_specs = (P("genes", "samples"), P("genes", "samples"))
    return jax.shard_map(
        on_device, mesh=mesh, in_specs=in_specs, out_specs=out_specs, check_vma=False
    )
```

profile of v0, /device:TPU:1, one launch (start us, length us, event | category | flops | bytes accessed | tf_op | source)
XLA Modules:
  0.0 588.2 jit_solution(16046461581918448854)
XLA Ops:
  7.2 0.7 broadcast_compare_fusion
  8.1 1.4 fusion.55
  9.6 0.8 convert_element_type.19
  10.7 1.9 mul.45
  12.7 0.6 mul.46
  13.3 0.7 multiply_add_fusion
  14.1 1.8 mul.47
  15.9 1.1 convolution_convert_fusion
  17.0 3.4 copy.54
  20.5 6.4 %all-to-all-start = ((bf16[128,24,512]{2,1,0:T(8,128)(2,1)}), bf16[128,24,512]{2,1,0:T(8,128)(2,1)S(1)}, u32[]{:S(2)}, u32[]{:S(2)}) async-start(bf16[128,24,512]{2,1,0:T(8,128)(2,1)} %copy.54), calls=%async_computation | async-start | bytes 6291456 | tf_op jit(solution)/shard_map/all_to_all | solution.py:49
  27.0 10.3 %gather_fusion.3 = bf16[128,512,128]{2,1,0:T(8,128)(2,1)} fusion(bf16[32,512,128]{2,1,0:T(8,128)(2,1)} %param.8, s32[1024]{0:T(1024)S(1)} %pad_clamp_fusion.2), kind=kCustom, calls=%fused_computation.2.clone | custom fusion | bytes 33554944 | tf_op jit(solution)/shard_map/jit(_take)/gather | solution.py:52
  37.4 10.4 %gather_fusion.2 = bf16[128,512,128]{2,1,0:T(8,128)(2,1)} fusion(bf16[32,512,128]{2,1,0:T(8,128)(2,1)} %param.8, s32[1024]{0:T(1024)S(1)} %pad_clamp_fusion.3), kind=kCustom, calls=%fused_computation.1.clone | custom fusion | bytes 33554944 | tf_op jit(solution)/shard_map/jit(_take)/gather | solution.py:52
  47.7 10.3 %gather_fusion.4 = bf16[128,512,128]{2,1,0:T(8,128)(2,1)} fusion(bf16[32,512,128]{2,1,0:T(8,128)(2,1)} %param.8, s32[1024]{0:T(1024)S(1)} %pad_clamp_fusion.1), kind=kCustom, calls=%fused_computation.3.clone | custom fusion | bytes 33554944 | tf_op jit(solution)/shard_map/jit(_take)/gather | solution.py:52
  58.0 10.3 %gather_fusion.1 = bf16[128,512,128]{2,1,0:T(8,128)(2,1)} fusion(bf16[32,512,128]{2,1,0:T(8,128)(2,1)} %param.8, s32[1024]{0:T(1024)S(1)} %pad_clamp_fusion.4), kind=kCustom, calls=%fused_computation.clone | custom fusion | bytes 33554944 | tf_op jit(solution)/shard_map/jit(_take)/gather | solution.py:52
  68.2 17.5 %fusion.2 = f32[128,24,512]{2,1,0:T(8,128)} fusion(bf16[128,512,128]{2,1,0:T(8,128)(2,1)} %gather_fusion.3, pred[128]{0:T(512)(128)(4,1)S(1)} %get-tuple-element.26, bf16[128,24,512]{2,1,0:T(8,128)(2,1)S(1)} %all-to-all-done), kind=kOutput, calls=%fused_computation.7 | convolution fusion | flops 411041792 | bytes 23855616 | tf_op jit(solution)/shard_map/csv,ctv->cts/dot_general | solution.py:54
  85.7 17.4 %fusion.4 = f32[128,24,512]{2,1,0:T(8,128)} fusion(bf16[128,512,128]{2,1,0:T(8,128)(2,1)} %gather_fusion.2, pred[128]{0:T(512)(128)(4,1)S(1)} %get-tuple-element.13, bf16[128,24,512]{2,1,0:T(8,128)(2,1)S(1)} %all-to-all-done), kind=kOutput, calls=%fused_computation.9 | convolution fusion | flops 411041792 | bytes 23855616 | tf_op jit(solution)/shard_map/csv,ctv->cts/dot_general | solution.py:54
  103.1 17.4 %fusion = f32[128,24,512]{2,1,0:T(8,128)} fusion(bf16[128,512,128]{2,1,0:T(8,128)(2,1)} %gather_fusion.4, pred[128]{0:T(512)(128)(4,1)S(1)} %get-tuple-element.28, bf16[128,24,512]{2,1,0:T(8,128)(2,1)S(1)} %all-to-all-done), kind=kOutput, calls=%fused_computation.5 | convolution fusion | flops 411041792 | bytes 23855616 | tf_op jit(solution)/shard_map/csv,ctv->cts/dot_general | solution.py:54
  120.4 17.0 %add_convert_fusion = bf16[128,24,512]{2,1,0:T(8,128)(2,1)} fusion(f32[128,24,512]{2,1,0:T(8,128)} %fusion, f32[128,24,512]{2,1,0:T(8,128)} %fusion.2, f32[128,24,512]{2,1,0:T(8,128)} %fusion.4, bf16[128,512,128]{2,1,0:T(8,128)(2,1)} %gather_fusion.1, pred[128]{0:T(512)(128)(4,1)S(1)} %get-tuple-element.25, bf16[128,24,512]{2,1,0:T(8,128)(2,1)S(1)} %all-to-all-done), kind=kOutput, calls=%fused_computation.21 | convolution fusion | flops 417333248 | bytes 39584256 | tf_op jit(solution)/shard_map/csv,ctv->cts/dot_general | solution.py:54
  137.4 5.3 all-to-all-start.1
  142.7 37.4 %all-to-all-done.1 = bf16[128,24,512]{2,1,0:T(8,128)(2,1)S(1)} async-done(((bf16[128,24,512]{2,1,0:T(8,128)(2,1)}), bf16[128,24,512]{2,1,0:T(8,128)(2,1)S(1)}, u32[]{:S(2)}, u32[]{:S(2)}) %all-to-all-start.1) | async-done | bytes 3145760 | tf_op jit(solution)/shard_map/all_to_all | solution.py:58
  180.1 1.8 gather_fusion
  181.9 6.6 %fusion.26 = f32[64,24,256]{1,2,0:T(8,128)} fusion(bf16[64,24,512]{2,1,0:T(8,128)(2,1)} %gather_fusion, pred[64]{0:T(512)(128)(4,1)S(1)} %get-tuple-element.11, bf16[512,256]{1,0:T(8,128)(2,1)S(1)} %copy-done), kind=kOutput, calls=%fused_computation.35 | convolution fusion | flops 403439616 | bytes 3407936 | tf_op jit(solution)/shard_map/dot_general | solution.py:61
  188.6 0.7 copy-done.2
  189.3 0.6 fusion.54
  191.2 89.7 %psum.15 = f32[64,24]{1,0:T(8,128)S(1)} all-reduce(f32[64,24]{1,0:T(8,128)S(1)} %multiply_reduce_fusion), channel_id=1, replica_groups=mesh['samples'=16,'genes'=8,'tissues'=2] {'samples'}, use_global_device_ids=true, to_apply=%region_6.8 | all-reduce | flops 1536 | bytes 12288 | tf_op jit(solution)/shard_map/psum | solution.py:66
  280.9 293.0 %all-reduce.2.cloned.1.call-done = f32[64,24,256]{1,2,0:T(8,128)} async-done(((f32[64,24,256]{1,2,0:T(8,128)}), f32[64,24,256]{1,2,0:T(8,128)}) %all-reduce.2.cloned.1.call-update) | async-done | bytes 1572880 | tf_op jit(solution)/shard_map/psum | solution.py:66
  573.9 1.1 dynamic-slice_divide_fusion
  575.2 2.8 all_gather.3
  578.1 0.7 fusion.20
  579.3 0.7 fusion.36
  580.0 0.7 copy.60
  580.7 0.7 copy.61
  (29 shorter events, 2.4 us)
Async XLA Ops:
  7.2 174.8 %copy-start = (bf16[512,256]{1,0:T(8,128)(2,1)S(1)}, bf16[512,256]{1,0:T(8,128)(2,1)}, u32[]{:S(2)}) copy-start(bf16[512,256]{1,0:T(8,128)(2,1)} %param.9) | copy-start | bytes 786436
  20.5 47.8 %all-to-all-start = ((bf16[128,24,512]{2,1,0:T(8,128)(2,1)}), bf16[128,24,512]{2,1,0:T(8,128)(2,1)S(1)}, u32[]{:S(2)}, u32[]{:S(2)}) async-start(bf16[128,24,512]{2,1,0:T(8,128)(2,1)} %copy.54), calls=%async_computation | async-start | bytes 6291456 | tf_op jit(solution)/shard_map/all_to_all | solution.py:49
  137.4 42.7 %all-to-all-start.1 = ((bf16[128,24,512]{2,1,0:T(8,128)(2,1)}), bf16[128,24,512]{2,1,0:T(8,128)(2,1)S(1)}, u32[]{:S(2)}, u32[]{:S(2)}) async-start(bf16[128,24,512]{2,1,0:T(8,128)(2,1)} %add_convert_fusion), calls=%async_computation.1 | async-start | bytes 6291456 | tf_op jit(solution)/shard_map/all_to_all | solution.py:58
  142.7 431.2 %all-reduce.2.cloned.1.call-start = ((), (), s32[]{:S(2)}) async-start(), calls=%async_computation.2 | async-start | bytes 16777216 | tf_op jit(solution)/shard_map/psum | solution.py:66
  188.5 0.7 copy-start.2
  188.5 2.0 copy-start.1
Sparse Core Ops, SparseCore 0:
  188.7 385.1 all-reduce.1
where the time goes:
time: 589 us; the launch traced here: 588 us
  waiting for transfers between devices  330 us (56%)
  blocking collectives  92.5 us (16%)
  matrix products  78 us (13%)
  local copies, waits for them, and re-layouts  52.1 us (9%)
  between operations  14.9 us (3%)
  starting transfers between devices  11.7 us (2%)
  other arithmetic  8.69 us (1%)
    psum x1, waiting for transfers between devices, on_device(): products, squares = lax.psum((products, squares), 'samples')  293 us
    psum x1, blocking collectives, on_device(): products, squares = lax.psum((products, squares), 'samples')  89.7 us
    dot_general x4, matrix products, on_device(): jnp.einsum('csv,ctv->cts', blocks, piece, preferred_element_type=jnp.floa...  69.2 us
    gather x4, local copies, waits for them, and re-layouts, on_device(): blocks = jnp.take(dosage, slot_offset + offset, axis=0)  41.2 us
    all_to_all x1, waiting for transfers between devices, on_device(): lax.all_to_all(predicted, 'genes', split_axis=0, concat_axis=0, tiled=True)  37.4 us
  transfers between devices with their start and end apart: 3, of which 2 were waited for; matrix products, arithmetic and copies ran while one was open for 7% of the time, Pallas kernels for 0%

commit v1 on v0

v1 whole, which is shorter than its diff:
```python
import jax
import jax.numpy as jnp
from jax import lax
from jax.experimental import pallas as pl
from jax.experimental.pallas import tpu as pltpu
from jax.sharding import PartitionSpec as P

TISSUES = 48
MESH = pl.DeviceIdType.MESH
F32 = jnp.float32
BF16 = jnp.bfloat16
RING = 4
WIN = 4
PAIR = 2 * WIN
PARTS = 2
HALVES = 2


def halve(value):
    high = value.astype(BF16)
    return high, (value - high.astype(F32)).astype(BF16)


def merge(target, sources):
    cross = [ref[:WIN].astype(F32) + ref[WIN:PAIR].astype(F32) for ref in sources]
    high, low = halve(sum(cross[1:], cross[0]))
    target[:WIN] = high
    target[WIN:PAIR] = low
    gram = [ref[PAIR:].astype(F32) for ref in sources]
    target[PAIR:] = sum(gram[1:], gram[0]).astype(BF16)


def merge_all(target, sources):
    if len(target.shape) == 3:
        merge(target, sources)
        return

    def step(i, carry):
        merge(target.at[i], [ref.at[i] for ref in sources])
        return carry

    lax.fori_loop(0, target.shape[0], step, 0)


def kernel(
    start_ref, dosage_ref, traits_ref, masked_ref, precision_ref, out_ref,
    flipped, traits_t, send, xin, ysum, zin, table, mine, squares, partial, received, prods, result,
    send_sem, recv_sem, local_sem,
):
    samples, genes, core = lax.axis_index("samples"), lax.axis_index("genes"), lax.axis_index("tissues")
    x, zh = samples // RING, samples % RING
    zl, y = genes // RING, genes % RING
    block_count = dosage_ref.shape[0]
    half_blocks = block_count // 2
    groups = half_blocks // WIN
    per_part = half_blocks // PARTS
    gene_half = mine.shape[0]
    kmine = table.shape[2]
    base = core * half_blocks

    def turn(value, by):
        return (value + by + RING) % RING

    def at_x(to):
        return {"samples": to * RING + zh, "genes": genes, "tissues": core}

    def at_z(to):
        return {"samples": x * RING + to, "genes": genes, "tissues": core}

    def at_y(to):
        return {"samples": samples, "genes": zl * RING + to, "tissues": core}

    twin = {"samples": samples, "genes": (1 - zl) * RING + y, "tissues": core}
    partner = {"samples": samples, "genes": genes, "tissues": 1 - core}

    barrier = pltpu.get_barrier_semaphore()
    peers = [at_x(turn(x, k)) for k in (1, 2, 3)] + [at_z(turn(zh, k)) for k in (1, 2, 3)]
    peers += [at_y(turn(y, 1)), at_y(turn(y, -1)), twin, partner]
    for peer in peers:
        pl.semaphore_signal(barrier, inc=1, device_id=peer, device_id_type=MESH)

    counter = [0]
    started = []

    def copy(src, dst, to):
        index = counter[0]
        counter[0] += 1
        made = pltpu.make_async_remote_copy(
            src_ref=src, dst_ref=dst, send_sem=send_sem.at[index], recv_sem=recv_sem.at[index],
            device_id=to, device_id_type=MESH,
        )
        made.start()
        started.append(made)
        return index

    def arrival(index, dst):
        pltpu.make_async_remote_copy(
            src_ref=dst, dst_ref=dst, send_sem=send_sem.at[index], recv_sem=recv_sem.at[index],
            device_id=partner, device_id_type=MESH,
        ).wait_recv()

    own_copy = pltpu.make_async_copy(
        masked_ref.at[pl.ds(core * gene_half, gene_half)], mine.at[:, :, core], local_sem.at[0]
    )
    own_copy.start()

    traits_t[...] = traits_ref[...].T

    def flip(i, carry):
        flipped[i] = dosage_ref[jnp.maximum(base + i - (WIN - 1), 0)].T
        return carry

    lax.fori_loop(0, half_blocks + WIN - 1, flip, 0)

    def compute(part):
        def step(i, carry):
            local = part * per_part + i
            group, j = local // WIN, local % WIN
            block = dosage_ref[base + local]
            high, low = halve(jnp.dot(traits_t[...], block, preferred_element_type=F32))
            high = high.reshape(RING, RING, kmine, block.shape[1])
            low = low.reshape(RING, RING, kmine, block.shape[1])
            for ix in range(RING):
                send[ix, group, :, j] = high[ix]
                send[ix, group, :, j + WIN] = low[ix]
            left = flipped[pl.ds(local, WIN)]
            left = left.reshape(WIN * left.shape[1], left.shape[2])
            gram = jnp.dot(left, block, preferred_element_type=F32).astype(BF16)
            gram = gram.reshape(WIN, block.shape[1] // kmine, kmine, block.shape[1])
            for d in range(WIN):
                send[j, group, d, PAIR:] = gram[WIN - 1 - d]
            return carry

        lax.fori_loop(0, per_part, step, 0)

    class Scatter:
        def __init__(self, part, chunk, landing, at, me):
            self.part, self.chunk, self.landing, self.at, self.me = part, chunk, landing, at, me
            self.right, self.left, self.far = turn(me, 1), turn(me, -1), turn(me, 2)

        def spot(self, half, kind):
            return self.landing.at[self.part, half, kind]

        def group(self, half):
            return self.part * HALVES + half

        def send_far(self):
            self.far0 = copy(self.chunk(self.far, self.group(0)), self.spot(0, 0), self.at(self.right))
            self.far1 = copy(self.chunk(self.far, self.group(1)), self.spot(1, 0), self.at(self.left))

        def send_near(self):
            self.near0 = copy(self.chunk(self.left, self.group(0)), self.spot(0, 2), self.at(self.left))
            self.near1 = copy(self.chunk(self.right, self.group(1)), self.spot(1, 2), self.at(self.right))

        def relay(self):
            for half, index, to in ((0, self.far0, self.right), (1, self.far1, self.left)):
                spot = self.spot(half, 0)
                arrival(index, spot)
                merge_all(spot, [spot, self.chunk(to, self.group(half))])
                index = copy(spot, self.spot(half, 1), self.at(to))
                if half == 0:
                    self.sum0 = index
                else:
                    self.sum1 = index

        def total(self, half, target):
            arrival((self.near0, self.near1)[half], self.spot(half, 2))
            arrival((self.sum0, self.sum1)[half], self.spot(half, 1))
            merge_all(target, [self.chunk(self.me, self.group(half)), self.spot(half, 1), self.spot(half, 2)])

    xs = [Scatter(p, lambda to, group: send.at[to, group], xin, at_x, x) for p in range(PARTS)]
    zs = [Scatter(p, lambda to, group: ysum.at[group, to], zin, at_z, zh) for p in range(PARTS)]

    def slot(gene_index, part):
        return (gene_index * 2 + core) * groups + part * HALVES

    def other_slot(gene_index, part):
        return (gene_index * 2 + 1 - core) * groups + part * HALVES

    arrivals = []

    def to_partner(gene_index, part, half=None):
        first = slot(gene_index, part) + (half or 0)
        size = HALVES if half is None else 1
        ref = table.at[pl.ds(first, size)]
        index = copy(ref, ref, partner)
        arrivals.append((index, table.at[pl.ds(other_slot(gene_index, part) + (half or 0), size)]))

    class Gather:
        def __init__(self, part):
            self.part = part

        def chunk(self, gene_index, half=None):
            if half is None:
                return table.at[pl.ds(slot(gene_index, self.part), HALVES)]
            return table.at[pl.ds(slot(gene_index, self.part) + half, 1)]

        def send_y(self, gene_index):
            ref = self.chunk(gene_index)
            return copy(ref, ref, at_y(turn(y, 1))), copy(ref, ref, at_y(turn(y, -1)))

        def begin(self):
            for half in range(HALVES):
                zs[self.part].total(half, table.at[slot(genes, self.part) + half])
            own = self.chunk(genes)
            self.twin = copy(own, own, twin)
            self.first = self.send_y(genes)
            to_partner(genes, self.part)

        def middle(self):
            other = (1 - zl) * RING + y
            arrival(self.twin, self.chunk(other))
            self.second = self.send_y(other)
            to_partner(other, self.part)

        def forward(self, zone, indices):
            fromleft, fromright = zone * RING + turn(y, -1), zone * RING + turn(y, 1)
            arrival(indices[0], self.chunk(fromleft))
            ref = self.chunk(fromleft, 0)
            onward0 = copy(ref, ref, at_y(turn(y, 1)))
            to_partner(fromleft, self.part)
            arrival(indices[1], self.chunk(fromright))
            ref = self.chunk(fromright, 1)
            onward1 = copy(ref, ref, at_y(turn(y, -1)))
            to_partner(fromright, self.part)
            return onward0, onward1

        def finish(self, zone, onward):
            far = zone * RING + turn(y, 2)
            for half in range(HALVES):
                arrival(onward[half], self.chunk(far, half))
                to_partner(far, self.part, half)

        def spread(self):
            self.onward0 = self.forward(zl, self.first)
            self.onward1 = self.forward(1 - zl, self.second)

        def end(self):
            self.finish(zl, self.onward0)
            self.finish(1 - zl, self.onward1)

    gs = [Gather(p) for p in range(PARTS)]

    def x_total(part):
        for half in range(HALVES):
            xs[part].total(half, ysum.at[part * HALVES + half])
        zs[part].send_far()
        zs[part].send_near()

    compute(0)
    pl.semaphore_wait(barrier, len(peers))
    xs[0].send_far()
    xs[0].send_near()
    half_sent = copy(masked_ref.at[pl.ds((1 - core) * gene_half, gene_half)], mine.at[:, :, core], partner)
    compute(1)
    xs[1].send_far()
    xs[0].relay()
    xs[1].send_near()
    xs[1].relay()
    x_total(0)
    zs[0].relay()
    x_total(1)
    gs[0].begin()
    zs[1].relay()
    gs[0].middle()
    gs[0].spread()
    gs[1].begin()
    gs[1].middle()
    gs[0].end()
    gs[1].spread()
    gs[1].end()
    own_copy.wait()
    arrival(half_sent, mine.at[:, :, 1 - core])
    for index, ref in arrivals:
        arrival(index, ref)

    rows = mine.shape[2] * mine.shape[3]
    width = mine.shape[4]
    lanes = lax.broadcasted_iota(jnp.int32, (rows, width), 1)
    first_gene = (genes * 2 + core) * gene_half
    twice = jnp.where(zh == 0, 1.0, 2.0).astype(F32)
    squares[...] = jnp.zeros_like(squares)

    def square_step(g, carry):
        start = start_ref[first_gene + g]
        offset = (x + WIN - start % WIN) % WIN
        back = jnp.maximum(offset - zh, 0)
        scale = jnp.where(offset >= zh, twice, 0.0)
        pair = table[(start + offset) // WIN, PAIR:].reshape(width, width)
        near = mine[g, back].reshape(rows, width)
        far = mine[g, offset].reshape(rows, width)
        applied = jnp.dot(near, pair, preferred_element_type=F32) * far.astype(F32)
        total = jnp.sum(applied, axis=1, keepdims=True) * scale
        squares[...] += jnp.where(lanes == g, total, 0.0)
        return carry

    lax.fori_loop(0, gene_half, square_step, 0, unroll=8)

    def swap(stage, source, at, me):
        return [copy(source, received.at[stage, k - 1], at(turn(me, k))) for k in (1, 2, 3)]

    x_swap = swap(0, squares, at_x, x)

    def product_group(group, carry):
        for j in range(8):
            g = group * 8 + j
            start = start_ref[first_gene + g]
            spots = [((start + w) // WIN, (start + w) % WIN) for w in range(WIN)]
            tiles = [table[at, tile] for at, tile in spots]
            tiles += [table[at, tile + WIN] for at, tile in spots]
            rights = jnp.concatenate(tiles, axis=1)
            lefts = jnp.concatenate([mine[g, w].reshape(rows, width) for w in range(WIN)] * 2, axis=1)
            prods[group, :, j * kmine:(j + 1) * kmine] = lax.dot_general(
                lefts, rights, (((1,), (1,)), ((), ())), preferred_element_type=F32
            )
        return carry

    chunk_groups = gene_half // 8
    lax.fori_loop(0, chunk_groups // 2, product_group, 0)
    for k, index in enumerate(x_swap):
        arrival(index, received.at[0, k])
    partial[...] = squares[...] + received[0, 0] + received[0, 1] + received[0, 2]
    z_swap = swap(1, partial, at_z, zh)
    lax.fori_loop(chunk_groups // 2, chunk_groups, product_group, 0)
    for k, index in enumerate(z_swap):
        arrival(index, received.at[1, k])
    total = partial[...] + received[1, 0] + received[1, 1] + received[1, 2]

    columns = gene_half * kmine
    root = jnp.sqrt(jnp.maximum(total, 0.0) + 1.0)
    spread_rows = lax.broadcasted_iota(jnp.int32, (width, columns), 0)
    spread_cols = lax.broadcasted_iota(jnp.int32, (width, columns), 1)
    spread = (spread_rows == spread_cols // kmine).astype(F32)
    roots = jnp.dot(root, spread, preferred_element_type=F32, precision=lax.Precision.HIGHEST)
    products = jnp.concatenate([prods[i] for i in range(chunk_groups)], axis=1)
    scores = products / roots
    matrix = precision_ref[...]
    row_sums = jnp.sum(matrix, axis=1, keepdims=True)
    grand_total = jnp.sum(row_sums, axis=0, keepdims=True)
    weighted = jnp.dot(matrix, scores, preferred_element_type=F32, precision=lax.Precision.HIGHEST)
    linear = jnp.sum(row_sums * scores, axis=0, keepdims=True)
    quadratic = jnp.sum(scores * weighted, axis=0, keepdims=True)
    combined = linear / jnp.sqrt(grand_total)
    heterogeneity = (quadratic - linear * linear / grand_total) / TISSUES
    row = lax.broadcasted_iota(jnp.int32, (8, columns), 0)
    result[core] = jnp.where(row == 0, combined, heterogeneity)
    last = copy(result.at[core], result.at[core], partner)
    arrival(last, result.at[1 - core])
    out_ref[...] = result[...]
    for made in started:
        made.wait_send()


def on_device(dosage, traits, weights, block_mask, window_start, precision_matrix):
    block_count, sample_rows, block_len = dosage.shape
    gene_rows, tissue_cols, _ = weights.shape
    window_len = block_mask.shape[2]
    padded = (tissue_cols + 15) // 16 * 16
    ring_count = lax.axis_size("samples")
    trait_cols = traits.shape[1] // ring_count
    owners = lax.axis_size("genes")
    gene_half = gene_rows // 2
    shaped = weights.reshape(gene_rows, tissue_cols, window_len, block_len)
    masked = shaped * block_mask[..., None].astype(BF16)
    masked = jnp.transpose(masked, (0, 2, 1, 3))
    masked = jnp.pad(masked, ((0, 0), (0, 0), (0, padded - tissue_cols), (0, 0)))
    matrix = precision_matrix.reshape(2, tissue_cols, 2, tissue_cols)
    pad = (0, padded - tissue_cols)
    matrix = jnp.pad(matrix, ((0, 0), pad, (0, 0), pad)).reshape(2 * padded, 2 * padded)

    half_blocks = block_count // 2
    groups = half_blocks // WIN
    tiles = PAIR + block_len // trait_cols
    unit = (tiles, trait_cols, block_len)
    rows = 2 * padded
    columns = gene_half * trait_cols
    vmem = pl.BlockSpec(memory_space=pltpu.VMEM)
    copies = PARTS * (6 + 6 + 9 + 10) + 8
    out = pl.pallas_call(
        kernel,
        out_shape=jax.ShapeDtypeStruct((2, 8, columns), F32),
        in_specs=[pl.BlockSpec(memory_space=pltpu.SMEM), vmem, vmem, vmem, vmem],
        out_specs=vmem,
        scratch_shapes=[
            pltpu.VMEM((half_blocks + WIN - 1, block_len, sample_rows), BF16),
            pltpu.VMEM((traits.shape[1], sample_rows), BF16),
            pltpu.VMEM((RING, groups, RING) + unit, BF16),
            pltpu.VMEM((PARTS, HALVES, 3, RING) + unit, BF16),
            pltpu.VMEM((groups, RING) + unit, BF16),
            pltpu.VMEM((PARTS, HALVES, 3) + unit, BF16),
            pltpu.VMEM((owners * 2 * groups,) + unit, BF16),
            pltpu.VMEM((gene_half, window_len, 2, padded, block_len), BF16),
            pltpu.VMEM((rows, block_len), F32),
            pltpu.VMEM((rows, block_len), F32),
            pltpu.VMEM((2, 3, rows, block_len), F32),
            pltpu.VMEM((gene_half // 8, rows, 8 * trait_cols), F32),
            pltpu.VMEM((2, 8, columns), F32),
            pltpu.SemaphoreType.DMA((copies,)),
            pltpu.SemaphoreType.DMA((copies,)),
            pltpu.SemaphoreType.DMA((1,)),
        ],
        compiler_params=pltpu.CompilerParams(
            collective_id=0, has_side_effects=True, vmem_limit_bytes=60 * 1024 * 1024
        ),
        name="twas",
    )(window_start, dosage, traits, masked, matrix)
    combined = out[:, 0, :].reshape(gene_rows, trait_cols)
    heterogeneity = out[:, 1, :].reshape(gene_rows, trait_cols)
    return (combined, heterogeneity)


def solution(mesh):
    in_specs = (
        P("genes", "samples", None),
        P("samples", None),
        P("genes", "tissues", None),
        P("genes", "tissues", None),
        P(),
        P(),
    )
    out_specs = (P("genes", "samples"), P("genes", "samples"))
    return jax.shard_map(
        on_device, mesh=mesh, in_specs=in_specs, out_specs=out_specs, check_vma=False
    )
```

time: 589 us -> 104 us (0.18)
  waiting for transfers between devices: 330 us -> 0 us
  Pallas kernels: 0 us -> 95.8 us
  blocking collectives: 92.5 us -> 0 us
  matrix products: 78 us -> 0 us
  local copies, waits for them, and re-layouts: 52.1 us -> 5.63 us
  between operations: 14.9 us -> 0.68 us
  starting transfers between devices: 11.7 us -> 0 us
  other arithmetic: 8.69 us -> 1.89 us
    psum x1 -> x0, waiting for transfers between devices: 293 us -> none  [on_device(): products, squares = lax.psum((products, squares), 'samples')]
    pallas_call x0 -> x1, Pallas kernels: none -> 95.8 us  [on_device(): pl.pallas_call(kernel, out_shape=jax.ShapeDtypeStruct((2, 8, columns), F3...]
    psum x1 -> x0, blocking collectives: 89.7 us -> none  [on_device(): products, squares = lax.psum((products, squares), 'samples')]
    dot_general x8 -> x0, matrix products: 78 us -> none  [the longest x4 69.2 us: on_device(): jnp.einsum('csv,ctv->cts', blocks, piece, preferred_element_type=jnp.floa...]
    gather x5 -> x0, local copies, waits for them, and re-layouts: 43 us -> none  [the longest x4 41.2 us: on_device(): blocks = jnp.take(dosage, slot_offset + offset, axis=0)]
    all_to_all x2 -> x0, waiting for transfers between devices: 37.4 us -> none  [the longest x1 37.4 us: on_device(): lax.all_to_all(predicted, 'genes', split_axis=0, concat_axis=0, tiled=True)]
    all_to_all x2 -> x0, starting transfers between devices: 11.6 us -> none  [the longest x1 6.36 us: on_device(): lax.all_to_all(outgoing, 'genes', split_axis=0, concat_axis=0, tiled=True)]
  transfers between devices with their start and end apart: 3 -> 0, of which waited for: 2 -> 0; matrix products, arithmetic and copies ran while one was open for 7% -> 0% of each run, Pallas kernels for 0% -> 0%
where the time goes in v1:
time: 104 us
  Pallas kernels  95.8 us (92%)
  local copies, waits for them, and re-layouts  5.63 us (5%)
  other arithmetic  1.89 us (2%)
    pallas_call x1, Pallas kernels, on_device(): pl.pallas_call(kernel, out_shape=jax.ShapeDtypeStruct((2, 8, columns), F3...  95.8 us

profile of v1, /device:TPU:1, one launch (start us, length us, event | category | flops | bytes accessed | tf_op | source)
XLA Modules:
  0.0 104.0 jit_solution(6328056950715247017)
XLA Ops:
  0.6 0.0 copy-start
  0.6 0.9 convert_element_type.8
  1.6 0.1 copy.11
  1.7 0.4 copy-done
  2.1 1.0 fusion
  3.0 0.0 copy-start.1
  3.0 1.9 %pad.8.masked_ref = bf16[64,4,32,128]{3,2,1,0:T(8,128)(2,1)} pad(bf16[64,4,24,128]{3,2,1,0:T(8,128)(2,1)S(1)} %fusion, bf16[]{:T(256)} %constant.3.clone.1), padding=0_0x0_0x0_8x0_0 | pad | bytes 3670018 | tf_op jit(solution)/shard_map/jit(_pad)/pad | solution.py:366
  5.0 0.0 copy-done.1
  5.0 0.1 reshape.16
  5.1 0.7 reshape.17.precision_ref
  5.8 95.8 %twas.1 = f32[2,8,512]{2,1,0:T(8,128)} custom-call(s32[512]{0:T(512)} %start_ref.1, bf16[32,512,128]{2,1,0:T(8,128)(2,1)} %dosage_ref.1, bf16[512,256]{1,0:T(8,128)(2,1)} %traits_ref.1, bf16[64,4,32,128]{3,2,1,0:T(8,128)(2,1)} %pad.8.masked_ref, f32[64,64]{1,0:T(8,128)} %reshape.17.precision_ref), custom_call_target="tpu_custom_call" | custom-call | tf_op jit(solution)/shard_map/twas/pallas_call | solution.py:379
  101.7 0.9 slice_reduce_fusion
  102.5 0.1 reshape_squeeze.6
  102.6 0.7 copy.13
  103.3 0.1 reshape_squeeze.7
  103.4 0.7 copy.14
  (1 shorter events, 0.0 us)
Async XLA Ops:
  0.6 1.4 %copy-start = (bf16[64,24,512]{2,1,0:T(8,128)(2,1)S(1)}, bf16[64,24,512]{2,1,0:T(8,128)(2,1)}, u32[]{:S(2)}) copy-start(bf16[64,24,512]{2,1,0:T(8,128)(2,1)} %param.8) | copy-start | bytes 4718596
  3.0 1.9 %copy-start.1 = (f32[48,48]{1,0:T(8,128)S(1)}, f32[48,48]{1,0:T(8,128)}, u32[]{:S(2)}) copy-start(f32[48,48]{1,0:T(8,128)} %param.11) | copy-start | bytes 27652
